TPU v7x, 32 devices: a whole 2x2x4 slice. The times are simulated.
32 devices in a mesh: dp: 16 (over z, x, core), mp: 2 (over y).
Axes of the slice: x: 2, y: 2, z: 4, core: 2. Of those that a mesh axis runs over, the one named last changes fastest.
Arguments:
- hidden_in: bfloat16 [16, 512, 768], P('dp', 'mp'), may hold values from -6 to 6
- memory: bfloat16 [16, 512, 768], P('dp', 'mp'), may hold values from -6 to 6
- cotangent: bfloat16 [16, 512, 768], P('dp', 'mp'), may hold values from -6 to 6
- self_query: bfloat16 [768, 768], P(None, 'mp'), may hold values from -0.0546875 to 0.0546875
- self_keyval: bfloat16 [2, 768, 768], P(None, None, 'mp'), may hold values from -0.21875 to 0.21875
- self_output: bfloat16 [768, 768], P('mp'), may hold values from -1.75 to 1.75
- cross_query: bfloat16 [768, 768], P(None, 'mp'), may hold values from -0.0546875 to 0.0546875
- cross_keyval: bfloat16 [2, 768, 768], P(None, None, 'mp'), may hold values from -0.21875 to 0.21875
- cross_output: bfloat16 [768, 768], P('mp'), may hold values from -2.5 to 2.5
- ffn_input: bfloat16 [2, 768, 2048], P(None, None, 'mp'), may hold values from -0.21875 to 0.21875
- ffn_output: bfloat16 [2048, 768], P('mp'), may hold values from -0.125 to 0.125
- norm_gains: bfloat16 [3, 768], replicated, may hold values from 0.5 to 1.5
- rel_bias: bfloat16 [32, 12], P(None, 'mp'), may hold values from -2.5 to 2.5
- dec_segments: int32 [16, 512], P('dp'), may hold values from 0 to 3, as said below
- mem_segments: int32 [16, 512], P('dp'), may hold values from 0 to 3, as said below
- rel_bucket: int32 [512], replicated, may hold values from 0 to 31, as said below
Outputs:
- output: bfloat16 [16, 512, 768], P('dp', 'mp')
- grad_input: float32 [16, 512, 768], P('dp', 'mp')
- grad_memory: float32 [16, 512, 768], P('dp', 'mp')
- grad_self_query: float32 [768, 768], P('dp', 'mp')
- grad_self_keyval: float32 [2, 768, 768], P(None, 'dp', 'mp')
- grad_self_output: float32 [768, 768], P('mp', 'dp')
- grad_cross_query: float32 [768, 768], P('dp', 'mp')
- grad_cross_keyval: float32 [2, 768, 768], P(None, 'dp', 'mp')
- grad_cross_output: float32 [768, 768], P('mp', 'dp')
- grad_ffn_input: float32 [2, 768, 2048], P(None, 'dp', 'mp')
- grad_ffn_output: float32 [2048, 768], P('mp', 'dp')
- grad_norm_gains: float32 [3, 768], replicated
- grad_rel_bias: float32 [32, 12], replicated
Inputs may be any that keep to these rules, and one draw needn't show every extreme that they name: `dec_segments`: in each row the ids never fall, start at 0 and take every value; one document holds both positions 255 and 256. `mem_segments`: in each row the ids never fall, start at 0 and take every value; one document holds both positions 255 and 256. `rel_bucket`: never falls along the distance, is 0 at distance 0, and takes every bucket.
All inputs are finite; a program needn't handle non-finite values.
Results may differ from a plain program's by a relative error of at most 0.029.
The roundings to bfloat16 on the way count: a program that leaves them out, or rounds other values in their place, can miss the bound.
Values may be sent and summed in bfloat16 or wider, within the bound.
No kernel may reach another device: no remote copies, remote signals or barrier semaphores. Data moves between devices by JAX's collectives and lax.ppermute only.
A program may use at most 192 MiB of HBM per device.

v0:
```python
import jax
import jax.numpy as jnp
from jax import lax
from jax.sharding import PartitionSpec as P

epsilon = 1e-06
masked_score = -1e30


def rms_norm(values, gain):
    scale = lax.rsqrt(jnp.mean(values * values, axis=-1, keepdims=True) + epsilon)
    return values * scale * gain


def norm_back(values, gain, grad):
    _, pull = jax.vjp(rms_norm, values, gain)
    return pull(grad)


def gated(gate_part, up_part):
    return jax.nn.gelu(gate_part, approximate=True) * up_part


def by_heads(values, heads):
    return values.reshape(values.shape[0], heads, values.shape[1] // heads)


def scores_of(query, keys, extra, allowed):
    scores = jnp.einsum("qhd,khd->hqk", query, keys, preferred_element_type=jnp.float32) + extra
    return jnp.where(allowed[None], scores, masked_score)


def attend_row(query, keys, values, extra, allowed):
    scores = scores_of(query, keys, extra, allowed)
    top = jnp.max(scores, axis=-1, keepdims=True)
    weights = jnp.exp(scores - top)
    total = jnp.sum(weights, axis=-1, keepdims=True)
    probs = (weights / total).astype(jnp.bfloat16)
    context = jnp.einsum("hqk,khd->qhd", probs, values, preferred_element_type=jnp.float32)
    return (context.reshape(context.shape[0], -1).astype(jnp.bfloat16), top, total)


def attend_back(query, keys, values, extra, allowed, top, total, grad_context):
    scores = scores_of(query, keys, extra, allowed)
    probs = jnp.exp(scores - top) / total
    grad_probs = jnp.einsum(
        "qhd,khd->hqk", grad_context, values, preferred_element_type=jnp.float32
    )
    delta = jnp.sum(probs * grad_probs, axis=-1, keepdims=True)
    grad_scores = (probs * (grad_probs - delta)).astype(jnp.bfloat16)
    grad_query = jnp.einsum("hqk,khd->qhd", grad_scores, keys, preferred_element_type=jnp.float32)
    grad_keys = jnp.einsum("hqk,qhd->khd", grad_scores, query, preferred_element_type=jnp.float32)
    grad_values = jnp.einsum(
        "hqk,qhd->khd", probs.astype(jnp.bfloat16), grad_context, preferred_element_type=jnp.float32
    )
    query_rows = query.shape[0]
    key_rows = keys.shape[0]
    return (
        grad_query.reshape(query_rows, -1).astype(jnp.bfloat16),
        grad_keys.reshape(key_rows, -1),
        grad_values.reshape(key_rows, -1),
        grad_scores,
    )


def gather_normed(values):
    return lax.all_gather(values, "mp", axis=1, tiled=True)


def gather_grads(values):
    return lax.all_gather(values, "mp", axis=1, tiled=True)


def branch_total(values):
    return lax.psum_scatter(values, "mp", scatter_dimension=1, tiled=True)


def input_total(values):
    return lax.psum_scatter(
        values.astype(jnp.bfloat16), "mp", scatter_dimension=1, tiled=True
    ).astype(jnp.float32)


def body(
    hidden_in,
    memory,
    cotangent,
    self_query,
    self_keyval,
    self_output,
    cross_query,
    cross_keyval,
    cross_output,
    ffn_input,
    ffn_output,
    norm_gains,
    rel_bias,
    dec_segments,
    mem_segments,
    rel_bucket,
):
    length = dec_segments.shape[1]
    local_heads = rel_bias.shape[1]
    buckets = rel_bias.shape[0]
    gain_values = norm_gains.astype(jnp.float32)
    first_in = hidden_in.astype(jnp.float32)
    normed_one = rms_norm(first_in, gain_values[0]).astype(jnp.bfloat16)
    gathered_one = gather_normed(normed_one)
    query_rows = gathered_one.shape[1]
    query_pos = jnp.arange(query_rows, dtype=jnp.int32)
    key_pos = jnp.arange(length, dtype=jnp.int32)
    distance = jnp.clip(query_pos[:, None] - key_pos[None, :], 0, length - 1)
    bucket_index = jnp.take(rel_bucket, distance, axis=0)
    bucket_hot = (jnp.arange(buckets, dtype=jnp.int32)[:, None, None] == bucket_index[None]).astype(
        jnp.bfloat16
    )
    causal = query_pos[:, None] >= key_pos[None, :]
    bias_full = jnp.einsum("bij,bh->hij", bucket_hot, rel_bias, preferred_element_type=jnp.float32)

    def self_forward(items):
        query, keys, values, seg_ids, key_ids = items
        allowed = (seg_ids[:, None] == key_ids[None, :]) & causal
        return attend_row(
            by_heads(query, local_heads),
            by_heads(keys, local_heads),
            by_heads(values, local_heads),
            bias_full,
            allowed,
        )

    def cross_forward(items):
        query, keys, values, seg_ids, mem_ids = items
        allowed = seg_ids[:, None] == mem_ids[None, :]
        return attend_row(
            by_heads(query, local_heads),
            by_heads(keys, local_heads),
            by_heads(values, local_heads),
            0.0,
            allowed,
        )

    query_one = jnp.einsum(
        "rld,de->rle", gathered_one, self_query, preferred_element_type=jnp.float32
    ).astype(jnp.bfloat16)
    keyval_one = jnp.einsum(
        "rld,cde->crle", gathered_one, self_keyval, preferred_element_type=jnp.float32
    ).astype(jnp.bfloat16)
    context_one, top_one, total_one = lax.map(
        self_forward, (query_one, keyval_one[0], keyval_one[1], dec_segments, dec_segments)
    )
    after_self = first_in + branch_total(
        jnp.einsum("rle,ed->rld", context_one, self_output, preferred_element_type=jnp.float32)
    )
    normed_two = rms_norm(after_self, gain_values[1]).astype(jnp.bfloat16)
    gathered_two = gather_normed(normed_two)
    memory_all = lax.all_gather(memory, "mp", axis=1, tiled=True)
    query_two = jnp.einsum(
        "rld,de->rle", gathered_two, cross_query, preferred_element_type=jnp.float32
    ).astype(jnp.bfloat16)
    keyval_two = jnp.einsum(
        "rmd,cde->crme", memory_all, cross_keyval, preferred_element_type=jnp.float32
    ).astype(jnp.bfloat16)
    context_two, top_two, total_two = lax.map(
        cross_forward, (query_two, keyval_two[0], keyval_two[1], dec_segments, mem_segments)
    )
    after_cross = after_self + branch_total(
        jnp.einsum("rle,ed->rld", context_two, cross_output, preferred_element_type=jnp.float32)
    )
    normed_three = rms_norm(after_cross, gain_values[2]).astype(jnp.bfloat16)
    gathered_three = gather_normed(normed_three)
    gate_up = jnp.einsum(
        "rld,cdf->crlf", gathered_three, ffn_input, preferred_element_type=jnp.float32
    )
    hidden = gated(gate_up[0], gate_up[1]).astype(jnp.bfloat16)
    final = after_cross + branch_total(
        jnp.einsum("rlf,fd->rld", hidden, ffn_output, preferred_element_type=jnp.float32)
    )
    grad_out = cotangent.astype(jnp.float32)
    sent_three = gather_grads(cotangent)
    grad_ffn_output = jnp.einsum(
        "rlf,rld->fd", hidden, sent_three, preferred_element_type=jnp.float32
    )
    grad_hidden = jnp.einsum(
        "rld,fd->rlf", sent_three, ffn_output, preferred_element_type=jnp.float32
    )
    _, pull_gate = jax.vjp(gated, gate_up[0], gate_up[1])
    grad_gate, grad_upward = pull_gate(grad_hidden)
    grad_gate_up = jnp.stack([grad_gate, grad_upward]).astype(jnp.bfloat16)
    grad_ffn_input = jnp.einsum(
        "rld,crlf->cdf", gathered_three, grad_gate_up, preferred_element_type=jnp.float32
    )
    grad_normed_three = input_total(
        jnp.einsum("crlf,cdf->rld", grad_gate_up, ffn_input, preferred_element_type=jnp.float32)
    )
    grad_cross_in, gain_three = norm_back(after_cross, gain_values[2], grad_normed_three)
    grad_cross = grad_out + grad_cross_in
    sent_two = gather_grads(grad_cross.astype(jnp.bfloat16))
    grad_cross_output = jnp.einsum(
        "rle,rld->ed", context_two, sent_two, preferred_element_type=jnp.float32
    )
    grad_context_two = jnp.einsum(
        "rld,ed->rle", sent_two, cross_output, preferred_element_type=jnp.float32
    ).astype(jnp.bfloat16)

    def cross_backward(items):
        query, keys, values, seg_ids, mem_ids, top, total, grad_context = items
        allowed = seg_ids[:, None] == mem_ids[None, :]
        grad_query, grad_keys, grad_values, _ = attend_back(
            by_heads(query, local_heads),
            by_heads(keys, local_heads),
            by_heads(values, local_heads),
            0.0,
            allowed,
            top,
            total,
            by_heads(grad_context, local_heads),
        )
        return (grad_query, grad_keys, grad_values)

    grad_query_two, grad_key_two, grad_value_two = lax.map(
        cross_backward,
        (
            query_two,
            keyval_two[0],
            keyval_two[1],
            dec_segments,
            mem_segments,
            top_two,
            total_two,
            grad_context_two,
        ),
    )
    grad_keyval_two = jnp.stack([grad_key_two, grad_value_two])
    grad_keyval_two = grad_keyval_two.astype(jnp.bfloat16)
    grad_cross_query = jnp.einsum(
        "rld,rle->de", gathered_two, grad_query_two, preferred_element_type=jnp.float32
    )
    grad_cross_keyval = jnp.einsum(
        "rmd,crme->cde", memory_all, grad_keyval_two, preferred_element_type=jnp.float32
    )
    memory_terms = jnp.einsum(
        "crme,cde->rmd", grad_keyval_two, cross_keyval, preferred_element_type=jnp.float32
    )
    grad_memory = lax.psum_scatter(
        memory_terms.astype(jnp.bfloat16), "mp", scatter_dimension=1, tiled=True
    ).astype(jnp.float32)
    grad_normed_two = input_total(
        jnp.einsum("rle,de->rld", grad_query_two, cross_query, preferred_element_type=jnp.float32)
    )
    grad_self_in, gain_two = norm_back(after_self, gain_values[1], grad_normed_two)
    grad_self = grad_cross + grad_self_in
    sent_one = gather_grads(grad_self.astype(jnp.bfloat16))
    grad_self_output = jnp.einsum(
        "rle,rld->ed", context_one, sent_one, preferred_element_type=jnp.float32
    )
    grad_context_one = jnp.einsum(
        "rld,ed->rle", sent_one, self_output, preferred_element_type=jnp.float32
    ).astype(jnp.bfloat16)

    def self_backward(items):
        query, keys, values, seg_ids, key_ids, top, total, grad_context = items
        allowed = (seg_ids[:, None] == key_ids[None, :]) & causal
        grad_query, grad_keys, grad_values, grad_scores = attend_back(
            by_heads(query, local_heads),
            by_heads(keys, local_heads),
            by_heads(values, local_heads),
            bias_full,
            allowed,
            top,
            total,
            by_heads(grad_context, local_heads),
        )
        bias_part = jnp.einsum(
            "bij,hij->bh", bucket_hot, grad_scores, preferred_element_type=jnp.float32
        )
        return (grad_query, grad_keys, grad_values, bias_part)

    grad_query_one, grad_key_one, grad_value_one, bias_parts = lax.map(
        self_backward,
        (
            query_one,
            keyval_one[0],
            keyval_one[1],
            dec_segments,
            dec_segments,
            top_one,
            total_one,
            grad_context_one,
        ),
    )
    grad_keyval_one = jnp.stack([grad_key_one, grad_value_one])
    grad_keyval_one = grad_keyval_one.astype(jnp.bfloat16)
    grad_self_query = jnp.einsum(
        "rld,rle->de", gathered_one, grad_query_one, preferred_element_type=jnp.float32
    )
    grad_self_keyval = jnp.einsum(
        "rld,crle->cde", gathered_one, grad_keyval_one, preferred_element_type=jnp.float32
    )
    grad_normed_one = input_total(
        jnp.einsum("rle,de->rld", grad_query_one, self_query, preferred_element_type=jnp.float32)
        + jnp.einsum(
            "crle,cde->rld", grad_keyval_one, self_keyval, preferred_element_type=jnp.float32
        )
    )
    grad_first, gain_one = norm_back(first_in, gain_values[0], grad_normed_one)
    grad_input = grad_self + grad_first
    local_bias = jnp.sum(bias_parts, axis=0)
    full_bias = jnp.zeros((buckets, local_heads * lax.axis_size("mp")), jnp.float32)
    full_bias = lax.dynamic_update_slice(
        full_bias, local_bias, (jnp.int32(0), lax.axis_index("mp") * local_heads)
    )
    gain_sum, bias_sum = lax.psum(
        (jnp.stack([gain_one, gain_two, gain_three]), full_bias), ("dp", "mp")
    )
    local_grads = (
        grad_self_query[None],
        grad_self_keyval,
        grad_self_output,
        grad_cross_query[None],
        grad_cross_keyval,
        grad_cross_output,
        grad_ffn_input,
        grad_ffn_output,
    )
    summed = tuple(
        (
            lax.psum_scatter(local_grads[0], "dp", scatter_dimension=1, tiled=True),
            lax.psum_scatter(local_grads[1], "dp", scatter_dimension=1, tiled=True),
            lax.psum_scatter(local_grads[2], "dp", scatter_dimension=1, tiled=True),
            lax.psum_scatter(local_grads[3], "dp", scatter_dimension=1, tiled=True),
            lax.psum_scatter(local_grads[4], "dp", scatter_dimension=1, tiled=True),
            lax.psum_scatter(local_grads[5], "dp", scatter_dimension=1, tiled=True),
            lax.psum_scatter(local_grads[6], "dp", scatter_dimension=1, tiled=True),
            lax.psum_scatter(local_grads[7], "dp", scatter_dimension=1, tiled=True),
        )
    )
    return (
        final.astype(jnp.bfloat16),
        grad_input,
        grad_memory,
        summed[0][0],
        summed[1],
        summed[2],
        summed[3][0],
        summed[4],
        summed[5],
        summed[6],
        summed[7],
        gain_sum,
        bias_sum,
    )


def solution(mesh):
    in_specs = (
        P("dp", "mp", None),
        P("dp", "mp", None),
        P("dp", "mp", None),
        P(None, "mp"),
        P(None, None, "mp"),
        P("mp", None),
        P(None, "mp"),
        P(None, None, "mp"),
        P("mp", None),
        P(None, None, "mp"),
        P("mp", None),
        P(),
        P(None, "mp"),
        P("dp", None),
        P("dp", None),
        P(),
    )
    out_specs = (
        P("dp", "mp", None),
        P("dp", "mp", None),
        P("dp", "mp", None),
        P("dp", "mp"),
        P(None, "dp", "mp"),
        P("mp", "dp"),
        P("dp", "mp"),
        P(None, "dp", "mp"),
        P("mp", "dp"),
        P(None, "dp", "mp"),
        P("mp", "dp"),
        P(),
        P(),
    )
    return jax.shard_map(body, mesh=mesh, in_specs=in_specs, out_specs=out_specs, check_vma=False)
```

profile of v0, /device:TPU:0, one launch (start us, length us, event | category | flops | bytes accessed | tf_op | source)
XLA Modules:
  0.0 3644.8 jit_solution(5491428677398967052)
XLA Ops:
  11.9 12.8 all_gather.21
  29.0 2748.8 %gather_fusion = s32[262144]{0:T(1024)} fusion(s32[512]{0:T(512)S(1)} %copy-done.1, s32[262144]{0:T(1024)} %broadcast_clamp_fusion), kind=kCustom, calls=%fused_computation | custom fusion | bytes 3145728 | tf_op jit(solution)/shard_map/jit(_take)/gather | solution.py:113
  2782.5 7.2 fusion.3
  2789.7 9.2 copy.74
  2799.9 4.1 fusion.6
  2804.0 4.3 fusion.137
  2808.5 6.3 fusion.46
  2814.8 3.0 convolution_bitcast_fusion.5
  2817.9 16.2 all_gather.22
  2838.0 9.8 reduce-scatter.13.cloned.1.call-done
  2850.2 11.8 all_gather.23
  2864.1 6.7 fusion.138
  2870.8 3.5 fusion.52
  2877.0 17.3 all_gather.25
  2894.3 13.3 reduce-scatter.15.cloned.1.call-done
  2910.2 11.8 all_gather.24
  2931.5 17.8 reduce-scatter.19.cloned.1.call-done
  2953.8 11.7 all_gather.26
  2966.3 4.0 multiply_reduce_fusion.1
  2978.7 5.2 convolution_bitcast_fusion.6
  2984.0 4.8 fusion.55
  2990.8 3.9 convolution_convert_fusion.3
  2996.6 3.2 fusion.45
  3003.2 21.2 reduce-scatter.17.cloned.1.call-done
  3024.5 3.5 fusion.133
  3027.9 17.8 all_gather.27
  3046.6 4.0 multiply_reduce_fusion
  3051.3 3.5 multiply_convert_fusion
  3054.9 7.1 fusion.49
  3063.9 3.8 convolution_convert_fusion.4
  3075.1 6.2 convolution_bitcast_fusion
  3081.3 10.4 copy.93
  3091.7 3.6 convolution_bitcast_fusion.2
  3095.3 5.3 copy.91
  3100.5 3.6 convolution_bitcast_fusion.3
  3104.1 5.3 copy.89
  3109.5 2.9 fusion.94
  3115.7 5.5 fusion.62
  3121.3 3.0 fusion.91
  3129.1 7.8 copy.94
  3137.5 7.7 fusion.58
  3150.6 42.3 %all-reduce.3 = (f32[3,768]{1,0:T(4,128)}, f32[32,12]{0,1:T(8,128)}) all-reduce(f32[3,768]{1,0:T(4,128)S(1)} %pad_maximum_fusion.11, f32[32,12]{0,1:T(8,128)} %copy-done.38), channel_id=1, replica_groups=mesh['dp'=16,'mp'=2] {'dp','mp'}, use_global_device_ids=true, to_apply=%region_30.31 | all-reduce | flops 2688 | bytes 21504 | tf_op jit(solution)/shard_map/psum | solution.py:312
  3196.1 124.0 %all-reduce.7.cloned.1.call-done = (f32[2,768,384]{2,0,1:T(2,128)}, f32[2,768,384]{2,0,1:T(2,128)}, f32[2,768,1024]{2,0,1:T(2,128)}) async-done(((f32[2,768,384]{2,0,1:T(2,128)}, f32[2,768,384]{2,0,1:T(2,128)}, f32[2,768,1024]{2,0,1:T(2,128)}), (f32[2,768,384]{2,0,1:T(2,128)}, f32[2,768,384]{2,0,1:T(2,128)}, f32[2,768,1024]{2,0,1:T(2,128)})) %all-reduce.7.cloned.1.call-update) | async-done | bytes 11010064
  3324.4 58.5 %reduce-scatter.33.cloned.1.call-done = f32[384,48]{0,1:T(8,128)} async-done(((f32[384,768]{0,1:T(8,128)}), f32[384,48]{0,1:T(8,128)}) %reduce-scatter.33.cloned.1.call-update) | async-done | bytes 73744 | tf_op jit(solution)/shard_map/reduce_scatter | solution.py:332
  3382.9 61.6 %reduce-scatter.31.cloned.1.call-done = f32[1,48,384]{2,1,0:T(8,128)} async-done(((f32[1,768,384]{2,1,0:T(8,128)}), f32[1,48,384]{2,1,0:T(8,128)}) %reduce-scatter.31.cloned.1.call-update) | async-done | bytes 73744 | tf_op jit(solution)/shard_map/reduce_scatter | solution.py:330
  3444.5 70.2 %reduce-scatter.35.cloned.1.call-done = f32[1024,48]{0,1:T(8,128)} async-done(((f32[1024,768]{0,1:T(8,128)}), f32[1024,48]{0,1:T(8,128)}) %reduce-scatter.35.cloned.1.call-update) | async-done | bytes 196624 | tf_op jit(solution)/shard_map/reduce_scatter | solution.py:334
  3514.7 61.5 %reduce-scatter.29.cloned.1.call-done = f32[384,48]{0,1:T(8,128)} async-done(((f32[384,768]{0,1:T(8,128)}), f32[384,48]{0,1:T(8,128)}) %reduce-scatter.29.cloned.1.call-update) | async-done | bytes 73744 | tf_op jit(solution)/shard_map/reduce_scatter | solution.py:329
  3576.2 61.7 %reduce-scatter.27.cloned.1.call-done = f32[1,48,384]{2,1,0:T(8,128)} async-done(((f32[1,768,384]{2,1,0:T(8,128)}), f32[1,48,384]{2,1,0:T(8,128)}) %reduce-scatter.27.cloned.1.call-update) | async-done | bytes 73744 | tf_op jit(solution)/shard_map/reduce_scatter | solution.py:327
  (219 shorter events, 90.8 us)
Async XLA Ops:
  7.2 2915.7 %copy-start = (bf16[2,768,1024]{2,1,0:T(8,128)(2,1)S(1)}, bf16[2,768,1024]{2,1,0:T(8,128)(2,1)}, u32[]{:S(2)}) copy-start(bf16[2,768,1024]{2,1,0:T(8,128)(2,1)} %param.25) | copy-start | bytes 9437188
  7.2 2840.6 %reduce-scatter.13.cloned.1.call-start = ((), (), s32[]{:S(2)}) async-start(), calls=%async_computation.12 | async-start | bytes 2359296 | tf_op jit(solution)/shard_map/reduce_scatter | solution.py:75
  7.2 17.4 copy-start.27
  7.2 18.6 copy-start.52
  2777.8 4.7 copy-start.50
  2789.7 9.2 copy-start.48
  2789.7 9.2 copy-start.49
  2789.7 10.2 copy-start.12
  2804.0 4.5 copy-start.4
  2808.5 6.3 copy-start.35
  2817.9 30.0 copy-start.7
  2817.9 89.7 %reduce-scatter.15.cloned.1.call-start = ((), (), s32[]{:S(2)}) async-start(), calls=%async_computation.13 | async-start | bytes 2359296 | tf_op jit(solution)/shard_map/reduce_scatter | solution.py:75
  2835.0 15.1 copy-start.34
  2847.8 15.1 copy-start.24
  2849.2 21.6 copy-start.44
  2870.8 4.3 copy-start.22
  2876.9 33.1 copy-start.31
  2876.9 72.3 %reduce-scatter.19.cloned.1.call-start = ((), (), s32[]{:S(2)}) async-start(), calls=%async_computation.15 | async-start | bytes 1179648 | tf_op jit(solution)/shard_map/reduce_scatter | solution.py:79
  2931.4 68.5 %reduce-scatter.21.cloned.1.call-start = ((), (), s32[]{:S(2)}) async-start(), calls=%async_computation.16 | async-start | bytes 1179648 | tf_op jit(solution)/shard_map/reduce_scatter | solution.py:79
  2949.3 16.2 copy-start.23
  2949.3 17.1 copy-start.30
  2949.3 17.1 copy-start.43
  2952.1 13.8 copy-start.45
  2966.3 4.1 copy-start.53
  2966.3 4.1 slice-start.2
  2966.3 4.8 slice-start.3
  2978.7 45.8 %reduce-scatter.17.cloned.1.call-start = ((), (), s32[]{:S(2)}) async-start(), calls=%async_computation.14 | async-start | bytes 2359296 | tf_op jit(solution)/shard_map/reduce_scatter | solution.py:75
  2984.0 162.0 %reduce-scatter.25.cloned.1.call-start = ((), (), s32[]{:S(2)}) async-start(), calls=%async_computation.18 | async-start | bytes 1179648 | tf_op jit(solution)/shard_map/reduce_scatter | solution.py:244
  2999.8 148.1 %reduce-scatter.23.cloned.1.call-start = ((), (), s32[]{:S(2)}) async-start(), calls=%async_computation.17 | async-start | bytes 1179648 | tf_op jit(solution)/shard_map/reduce_scatter | solution.py:79
  3024.5 21.3 copy-start.26
  3024.5 22.1 copy-start.29
  3024.5 22.1 copy-start.36
  3046.2 4.4 copy-start.54
  3046.6 4.1 slice-start
  3046.6 4.7 slice-start.1
  3069.6 3.9 copy-start.28
  3075.0 245.0 %all-reduce.7.cloned.1.call-start = ((), (), s32[]{:S(2)}) async-start(), calls=%async_computation.24 | async-start | bytes 22020096
  3109.5 273.4 %reduce-scatter.33.cloned.1.call-start = ((), (), s32[]{:S(2)}) async-start(), calls=%async_computation.22 | async-start | bytes 1253376 | tf_op jit(solution)/shard_map/reduce_scatter | solution.py:332
  3112.5 332.0 %reduce-scatter.31.cloned.1.call-start = ((), (), s32[]{:S(2)}) async-start(), calls=%async_computation.21 | async-start | bytes 1253376 | tf_op jit(solution)/shard_map/reduce_scatter | solution.py:330
  3115.4 399.3 %reduce-scatter.35.cloned.1.call-start = ((), (), s32[]{:S(2)}) async-start(), calls=%async_computation.23 | async-start | bytes 3342336 | tf_op jit(solution)/shard_map/reduce_scatter | solution.py:334
  3121.2 6.0 copy-start.55
  3121.2 7.3 copy-start.41
  3121.3 454.9 %reduce-scatter.29.cloned.1.call-start = ((), (), s32[]{:S(2)}) async-start(), calls=%async_computation.20 | async-start | bytes 1253376 | tf_op jit(solution)/shard_map/reduce_scatter | solution.py:329
  3124.3 513.6 %reduce-scatter.27.cloned.1.call-start = ((), (), s32[]{:S(2)}) async-start(), calls=%async_computation.19 | async-start | bytes 1253376 | tf_op jit(solution)/shard_map/reduce_scatter | solution.py:327
  3129.1 7.8 copy-start.42
  3137.5 10.4 copy-start.33
  3137.5 10.4 copy-start.40
  3146.0 3.9 copy-start.38
  (28 other events, 45.2 us)
Sparse Core Ops, SparseCore 0:
  2818.0 29.7 reduce-scatter.12
  2877.1 30.4 reduce-scatter.14
  2931.5 17.6 reduce-scatter.18
  2978.8 17.4 reduce-scatter.20
  2998.3 26.0 reduce-scatter.16
  3026.6 22.4 reduce-scatter.24
  3075.2 17.4 reduce-scatter.22
  3109.6 210.4 all-reduce.6
  3324.7 58.1 reduce-scatter.32
  3387.4 57.0 reduce-scatter.30
  3449.3 65.2 reduce-scatter.34
  3519.2 56.9 reduce-scatter.28
  3580.8 57.0 reduce-scatter.26
where the time goes:
time: 3650 us; the launch traced here: 3640 us
  local copies, waits for them, and re-layouts  2820 us (77%)
  waiting for transfers between devices  500 us (14%)
  blocking collectives  141 us (4%)
  matrix products  128 us (4%)
  other arithmetic  38.7 us (1%)
    gather x2, local copies, waits for them, and re-layouts, body(): bucket_index = jnp.take(rel_bucket, distance, axis=0)  2750 us
    unnamed x14, waiting for transfers between devices  124 us
  transfers between devices with their start and end apart: 13, of which 10 were waited for; matrix products, arithmetic and copies ran while one was open for 4% of the time, Pallas kernels for 0%

commit v1 on v0

--- a/solution.py
+++ b/solution.py
@@ -110,7 +110,11 @@
     query_pos = jnp.arange(query_rows, dtype=jnp.int32)
     key_pos = jnp.arange(length, dtype=jnp.int32)
     distance = jnp.clip(query_pos[:, None] - key_pos[None, :], 0, length - 1)
-    bucket_index = jnp.take(rel_bucket, distance, axis=0)
+    starts = jnp.sum(
+        (rel_bucket[None, :] < jnp.arange(1, buckets, dtype=jnp.int32)[:, None]).astype(jnp.int32),
+        axis=1,
+    )
+    bucket_index = jnp.sum((distance[None] >= starts[:, None, None]).astype(jnp.int32), axis=0)
     bucket_hot = (jnp.arange(buckets, dtype=jnp.int32)[:, None, None] == bucket_index[None]).astype(
         jnp.bfloat16
     )

time: 3650 us -> 894 us (0.24)
  local copies, waits for them, and re-layouts: 2820 us -> 62.1 us
    gather x2 -> x0, local copies, waits for them, and re-layouts: 2750 us -> none  [body(): bucket_index = jnp.take(rel_bucket, distance, axis=0)]
  transfers between devices with their start and end apart: 13 -> 13, of which waited for: 10 -> 10; matrix products, arithmetic and copies ran while one was open for 4% -> 15% of each run, Pallas kernels for 0% -> 0%
where the time goes in v1:
time: 894 us; the launch traced here: 888 us
  waiting for transfers between devices  506 us (57%)
  blocking collectives  140 us (16%)
  matrix products  125 us (14%)
  local copies, waits for them, and re-layouts  62.1 us (7%)
  other arithmetic  38 us (4%)
  between operations  15.6 us (2%)
    unnamed x14, waiting for transfers between devices  127 us
    reduce_scatter x1, waiting for transfers between devices, body(): lax.psum_scatter(local_grads[7], 'dp', scatter_dimension=1, tiled=True)  70.2 us
    reduce_scatter x1, waiting for transfers between devices, body(): lax.psum_scatter(local_grads[0], 'dp', scatter_dimension=1, tiled=True)  61.7 us
    reduce_scatter x1, waiting for transfers between devices, body(): lax.psum_scatter(local_grads[3], 'dp', scatter_dimension=1, tiled=True)  61.6 us
    reduce_scatter x1, waiting for transfers between devices, body(): lax.psum_scatter(local_grads[2], 'dp', scatter_dimension=1, tiled=True)  61.5 us
    reduce_scatter x1, waiting for transfers between devices, body(): lax.psum_scatter(local_grads[5], 'dp', scatter_dimension=1, tiled=True)  58.5 us
    reduce_scatter x3, waiting for transfers between devices, branch_total(): return lax.psum_scatter(values, 'mp', scatter_dimension=1, tiled=True)  47.2 us
    all_gather x3, blocking collectives, gather_grads(): return lax.all_gather(values, 'mp', axis=1, tiled=True)  46.1 us
  transfers between devices with their start and end apart: 13, of which 10 were waited for; matrix products, arithmetic and copies ran while one was open for 15% of the time, Pallas kernels for 0%

profile of v1, /device:TPU:0, one launch (start us, length us, event | category | flops | bytes accessed | tf_op | source)
XLA Modules:
  0.0 887.7 jit_solution(10008397148960168755)
XLA Ops:
  10.7 12.8 %all_gather.21 = bf16[1,512,768]{2,1,0:T(8,128)(2,1)S(1)} all-gather(bf16[1,256,768]{2,1,0:T(8,128)(2,1)S(1)} %fusion.75), channel_id=1, replica_groups=mesh['dp'=16,'mp'=2] {'mp'}, dimensions={1}, use_global_device_ids=true | all-gather | bytes 1179648 | tf_op jit(solution)/shard_map/all_gather | solution.py:67
  26.6 3.2 convert_reduce_fusion
  30.8 7.4 fusion.3
  38.3 9.1 %copy.77 = f32[512,512,6]{0,1,2:T(8,128)} copy(f32[512,512,6]{1,2,0:T(8,128)} %fusion.3) | data formatting | bytes 12582912 | tf_op jit(solution)/shard_map/bij,bh->hij/dot_general | solution.py:122
  49.1 4.1 fusion.6
  53.2 4.8 fusion.132
  58.0 6.4 fusion.46
  64.4 3.0 convolution_bitcast_fusion.5
  67.5 15.2 %all_gather.22 = bf16[1,512,768]{2,1,0:T(8,128)(2,1)S(1)} all-gather(bf16[1,256,768]{2,1,0:T(8,128)(2,1)} %param.17), channel_id=1, replica_groups=mesh['dp'=16,'mp'=2] {'mp'}, dimensions={1}, use_global_device_ids=true | all-gather | bytes 1179648 | tf_op jit(solution)/shard_map/all_gather | solution.py:160
  86.7 10.2 %reduce-scatter.13.cloned.1.call-done = f32[1,256,768]{2,1,0:T(8,128)} async-done(((f32[1,512,768]{2,1,0:T(8,128)}), f32[1,256,768]{2,1,0:T(8,128)}) %reduce-scatter.13.cloned.1.call-update) | async-done | bytes 786448 | tf_op jit(solution)/shard_map/reduce_scatter | solution.py:75
  99.3 12.3 %all_gather.23 = bf16[1,512,768]{2,1,0:T(8,128)(2,1)S(1)} all-gather(bf16[1,256,768]{2,1,0:T(8,128)(2,1)S(1)} %multiply_convert_fusion.4), channel_id=1, replica_groups=mesh['dp'=16,'mp'=2] {'mp'}, dimensions={1}, use_global_device_ids=true | all-gather | bytes 1179648 | tf_op jit(solution)/shard_map/all_gather | solution.py:67
  113.8 6.7 fusion.133
  120.5 3.5 fusion.52
  126.7 17.3 %all_gather.25 = bf16[1,512,768]{2,1,0:T(8,128)(2,1)} all-gather(bf16[1,256,768]{2,1,0:T(8,128)(2,1)} %param.18), channel_id=1, replica_groups=mesh['dp'=16,'mp'=2] {'mp'}, dimensions={1}, use_global_device_ids=true | all-gather | bytes 1179648 | tf_op jit(solution)/shard_map/all_gather | solution.py:71
  144.0 13.3 %reduce-scatter.15.cloned.1.call-done = f32[1,256,768]{2,1,0:T(8,128)} async-done(((f32[1,512,768]{2,1,0:T(8,128)}), f32[1,256,768]{2,1,0:T(8,128)}) %reduce-scatter.15.cloned.1.call-update) | async-done | bytes 786448 | tf_op jit(solution)/shard_map/reduce_scatter | solution.py:75
  159.9 11.8 %all_gather.24 = bf16[1,512,768]{2,1,0:T(8,128)(2,1)S(1)} all-gather(bf16[1,256,768]{2,1,0:T(8,128)(2,1)S(1)} %multiply_convert_fusion.3), channel_id=1, replica_groups=mesh['dp'=16,'mp'=2] {'mp'}, dimensions={1}, use_global_device_ids=true | all-gather | bytes 1179648 | tf_op jit(solution)/shard_map/all_gather | solution.py:67
  181.1 17.8 %reduce-scatter.19.cloned.1.call-done = bf16[1,256,768]{2,1,0:T(8,128)(2,1)} async-done(((bf16[1,512,768]{2,1,0:T(8,128)(2,1)}), bf16[1,256,768]{2,1,0:T(8,128)(2,1)}) %reduce-scatter.19.cloned.1.call-update) | async-done | bytes 393232 | tf_op jit(solution)/shard_map/reduce_scatter | solution.py:79
  203.9 11.7 %all_gather.26 = bf16[1,512,768]{2,1,0:T(8,128)(2,1)S(1)} all-gather(bf16[1,256,768]{2,1,0:T(8,128)(2,1)S(1)} %fusion.108), channel_id=1, replica_groups=mesh['dp'=16,'mp'=2] {'mp'}, dimensions={1}, use_global_device_ids=true | all-gather | bytes 1179648 | tf_op jit(solution)/shard_map/all_gather | solution.py:71
  216.1 4.0 multiply_reduce_fusion.1
  225.7 5.3 convolution_bitcast_fusion.6
  231.1 4.8 fusion.55
  237.8 2.8 convolution_convert_fusion.3
  242.0 3.3 fusion.45
  247.8 23.6 %reduce-scatter.17.cloned.1.call-done = f32[1,256,768]{2,1,0:T(8,128)} async-done(((f32[1,512,768]{2,1,0:T(8,128)}), f32[1,256,768]{2,1,0:T(8,128)}) %reduce-scatter.17.cloned.1.call-update) | async-done | bytes 786448 | tf_op jit(solution)/shard_map/reduce_scatter | solution.py:75
  274.3 17.1 %all_gather.27 = bf16[1,512,768]{2,1,0:T(8,128)(2,1)S(1)} all-gather(bf16[1,256,768]{2,1,0:T(8,128)(2,1)S(1)} %get-tuple-element.204), channel_id=1, replica_groups=mesh['dp'=16,'mp'=2] {'mp'}, dimensions={1}, use_global_device_ids=true | all-gather | bytes 1179648 | tf_op jit(solution)/shard_map/all_gather | solution.py:71
  291.9 4.0 multiply_reduce_fusion
  298.6 7.2 fusion.49
  307.7 2.8 convolution_convert_fusion.4
  317.9 6.2 convolution_bitcast_fusion
  324.1 10.4 %copy.96 = f32[2,768,1024]{2,0,1:T(2,128)} copy(f32[2,768,1024]{1,2,0:T(8,128)} %convolution_bitcast_fusion) | data formatting | bytes 12582912 | tf_op jit(solution)/shard_map/rld,crlf->cdf/transpose | solution.py:193
  334.5 3.6 convolution_bitcast_fusion.2
  338.1 5.3 copy.94
  343.4 3.7 convolution_bitcast_fusion.3
  347.1 5.3 copy.92
  352.5 2.9 fusion.89
  355.5 2.9 convolution_bitcast_fusion.7
  358.6 5.5 fusion.61
  364.3 3.0 fusion.86
  367.3 2.9 convolution_bitcast_fusion.8
  372.1 5.6 copy.97
  378.3 7.0 fusion.58
  390.8 42.3 %all-reduce.3 = (f32[3,768]{1,0:T(4,128)}, f32[32,12]{0,1:T(8,128)}) all-reduce(f32[3,768]{1,0:T(4,128)} %pad_maximum_fusion.11, f32[32,12]{0,1:T(8,128)S(1)} %dynamic_update_slice.33), channel_id=1, replica_groups=mesh['dp'=16,'mp'=2] {'dp','mp'}, use_global_device_ids=true, to_apply=%region_32.33 | all-reduce | flops 2688 | bytes 21504 | tf_op jit(solution)/shard_map/psum | solution.py:316
  436.1 127.0 %all-reduce.7.cloned.1.call-done = (f32[2,768,384]{2,0,1:T(2,128)}, f32[2,768,384]{2,0,1:T(2,128)}, f32[2,768,1024]{2,0,1:T(2,128)}) async-done(((f32[2,768,384]{2,0,1:T(2,128)}, f32[2,768,384]{2,0,1:T(2,128)}, f32[2,768,1024]{2,0,1:T(2,128)}), (f32[2,768,384]{2,0,1:T(2,128)}, f32[2,768,384]{2,0,1:T(2,128)}, f32[2,768,1024]{2,0,1:T(2,128)})) %all-reduce.7.cloned.1.call-update) | async-done | bytes 11010064
  567.4 58.5 %reduce-scatter.33.cloned.1.call-done = f32[384,48]{0,1:T(8,128)} async-done(((f32[384,768]{0,1:T(8,128)}), f32[384,48]{0,1:T(8,128)}) %reduce-scatter.33.cloned.1.call-update) | async-done | bytes 73744 | tf_op jit(solution)/shard_map/reduce_scatter | solution.py:336
  625.9 61.6 %reduce-scatter.31.cloned.1.call-done = f32[1,48,384]{2,1,0:T(8,128)} async-done(((f32[1,768,384]{2,1,0:T(8,128)}), f32[1,48,384]{2,1,0:T(8,128)}) %reduce-scatter.31.cloned.1.call-update) | async-done | bytes 73744 | tf_op jit(solution)/shard_map/reduce_scatter | solution.py:334
  687.5 70.2 %reduce-scatter.35.cloned.1.call-done = f32[1024,48]{0,1:T(8,128)} async-done(((f32[1024,768]{0,1:T(8,128)}), f32[1024,48]{0,1:T(8,128)}) %reduce-scatter.35.cloned.1.call-update) | async-done | bytes 196624 | tf_op jit(solution)/shard_map/reduce_scatter | solution.py:338
  757.7 61.5 %reduce-scatter.29.cloned.1.call-done = f32[384,48]{0,1:T(8,128)} async-done(((f32[384,768]{0,1:T(8,128)}), f32[384,48]{0,1:T(8,128)}) %reduce-scatter.29.cloned.1.call-update) | async-done | bytes 73744 | tf_op jit(solution)/shard_map/reduce_scatter | solution.py:333
  819.2 61.7 %reduce-scatter.27.cloned.1.call-done = f32[1,48,384]{2,1,0:T(8,128)} async-done(((f32[1,768,384]{2,1,0:T(8,128)}), f32[1,48,384]{2,1,0:T(8,128)}) %reduce-scatter.27.cloned.1.call-update) | async-done | bytes 73744 | tf_op jit(solution)/shard_map/reduce_scatter | solution.py:331
  (219 shorter events, 79.4 us)
Async XLA Ops:
  7.2 165.4 %copy-start = (bf16[2,768,1024]{2,1,0:T(8,128)(2,1)S(1)}, bf16[2,768,1024]{2,1,0:T(8,128)(2,1)}, u32[]{:S(2)}) copy-start(bf16[2,768,1024]{2,1,0:T(8,128)(2,1)} %param.25) | copy-start | bytes 9437188
  7.2 89.7 %reduce-scatter.13.cloned.1.call-start = ((), (), s32[]{:S(2)}) async-start(), calls=%async_computation.12 | async-start | bytes 2359296 | tf_op jit(solution)/shard_map/reduce_scatter | solution.py:75
  7.2 16.2 %copy-start.31 = (bf16[768,384]{1,0:T(8,128)(2,1)S(1)}, bf16[768,384]{1,0:T(8,128)(2,1)}, u32[]{:S(2)}) copy-start(bf16[768,384]{1,0:T(8,128)(2,1)} %param.19) | copy-start | bytes 1769476
  7.3 17.5 %copy-start.53 = (bf16[2,768,384]{2,1,0:T(8,128)(2,1)S(1)}, bf16[2,768,384]{2,1,0:T(8,128)(2,1)}, u32[]{:S(2)}) copy-start(bf16[2,768,384]{2,1,0:T(8,128)(2,1)} %param.20) | copy-start | bytes 3538948
  24.7 6.1 copy-start.51
  26.4 22.7 %copy-start.14 = (bf16[1,1,512,384]{2,3,0,1:T(8,128)(2,1)}, bf16[1,1,512,384]{2,3,0,1:T(8,128)(2,1)S(1)}, u32[]{:S(2)}) copy-start(bf16[1,1,512,384]{2,3,0,1:T(8,128)(2,1)S(1)} %get-tuple-element.215) | copy-start | bytes 1179652
  38.3 9.1 %copy-start.49 = (s32[1,512]{1,0:T(1,128)S(1)}, s32[1,512]{1,0:T(1,128)}, u32[]{:S(2)}) copy-start(s32[1,512]{1,0:T(1,128)} %param.29) | copy-start | bytes 6148
  53.2 4.9 copy-start.2
  67.4 29.5 %copy-start.7 = (bf16[1,256,768]{2,1,0:T(8,128)(2,1)S(1)}, bf16[1,256,768]{2,1,0:T(8,128)(2,1)}, u32[]{:S(2)}) copy-start(bf16[1,256,768]{2,1,0:T(8,128)(2,1)} %param.16) | copy-start | bytes 1179652
  67.4 89.9 %reduce-scatter.15.cloned.1.call-start = ((), (), s32[]{:S(2)}) async-start(), calls=%async_computation.13 | async-start | bytes 2359296 | tf_op jit(solution)/shard_map/reduce_scatter | solution.py:75
  96.9 15.6 %copy-start.28 = (bf16[768,384]{1,0:T(8,128)(2,1)S(1)}, bf16[768,384]{1,0:T(8,128)(2,1)}, u32[]{:S(2)}) copy-start(bf16[768,384]{1,0:T(8,128)(2,1)} %param.22) | copy-start | bytes 1769476
  120.5 4.3 copy-start.26
  126.6 72.2 %reduce-scatter.19.cloned.1.call-start = ((), (), s32[]{:S(2)}) async-start(), calls=%async_computation.15 | async-start | bytes 1179648 | tf_op jit(solution)/shard_map/reduce_scatter | solution.py:79
  181.0 34.6 %copy-start.27 = (bf16[384,768]{1,0:T(8,128)(2,1)S(1)}, bf16[384,768]{1,0:T(8,128)(2,1)}, u32[]{:S(2)}) copy-start(bf16[384,768]{1,0:T(8,128)(2,1)} %param.24) | copy-start | bytes 1769476
  181.0 35.1 %copy-start.34 = (bf16[1,1,512,384]{2,3,0,1:T(8,128)(2,1)S(1)}, bf16[1,1,512,384]{2,3,0,1:T(8,128)(2,1)}, u32[]{:S(2)}) copy-start(bf16[1,1,512,384]{2,3,0,1:T(8,128)(2,1)} %get-tuple-element.214) | copy-start | bytes 1179652
  181.0 35.1 %copy-start.42 = (f32[6,512]{1,0:T(8,128)S(1)}, f32[6,512]{1,0:T(8,128)}, u32[]{:S(2)}) copy-start(f32[6,512]{1,0:T(8,128)} %get-tuple-element.221) | copy-start | bytes 36868
  181.1 64.3 %reduce-scatter.21.cloned.1.call-start = ((), (), s32[]{:S(2)}) async-start(), calls=%async_computation.16 | async-start | bytes 1179648 | tf_op jit(solution)/shard_map/reduce_scatter | solution.py:79
  215.6 4.6 copy-start.17
  216.1 4.1 slice-start.2
  216.1 4.8 slice-start.3
  216.1 4.8 copy-start.43
  225.7 45.8 %reduce-scatter.17.cloned.1.call-start = ((), (), s32[]{:S(2)}) async-start(), calls=%async_computation.14 | async-start | bytes 2359296 | tf_op jit(solution)/shard_map/reduce_scatter | solution.py:75
  231.0 154.4 %reduce-scatter.25.cloned.1.call-start = ((), (), s32[]{:S(2)}) async-start(), calls=%async_computation.18 | async-start | bytes 1179648 | tf_op jit(solution)/shard_map/reduce_scatter | solution.py:248
  240.6 4.8 copy-start.4
  240.6 4.8 copy-start.41
  240.6 6.6 copy-start.45
  240.6 30.9 %copy-start.6 = (f32[1,256,768]{2,1,0:T(8,128)S(1)}, f32[1,256,768]{2,1,0:T(8,128)}, u32[]{:S(2)}) copy-start(f32[1,256,768]{2,1,0:T(8,128)} %copy-done.5) | copy-start | bytes 2359300
  240.6 30.9 %copy-start.10 = (bf16[1,256,768]{2,1,0:T(8,128)(2,1)S(1)}, bf16[1,256,768]{2,1,0:T(8,128)(2,1)}, u32[]{:S(2)}) copy-start(bf16[1,256,768]{2,1,0:T(8,128)(2,1)} %param.18) | copy-start | bytes 1179652
  240.6 30.9 %copy-start.11 = (bf16[1,256,768]{2,1,0:T(8,128)(2,1)S(1)}, bf16[1,256,768]{2,1,0:T(8,128)(2,1)}, u32[]{:S(2)}) copy-start(bf16[1,256,768]{2,1,0:T(8,128)(2,1)} %reduce-scatter.19.cloned.1.call-done) | copy-start | bytes 1179652
  242.0 5.8 copy-start.22
  245.3 142.2 %reduce-scatter.23.cloned.1.call-start = ((), (), s32[]{:S(2)}) async-start(), calls=%async_computation.17 | async-start | bytes 1179648 | tf_op jit(solution)/shard_map/reduce_scatter | solution.py:79
  247.8 44.1 %copy-start.33 = (bf16[1,1,512,384]{2,3,0,1:T(8,128)(2,1)S(1)}, bf16[1,1,512,384]{2,3,0,1:T(8,128)(2,1)}, u32[]{:S(2)}) copy-start(bf16[1,1,512,384]{2,3,0,1:T(8,128)(2,1)} %get-tuple-element.216) | copy-start | bytes 1179652
  271.5 19.9 %copy-start.30 = (bf16[384,768]{1,0:T(8,128)(2,1)S(1)}, bf16[384,768]{1,0:T(8,128)(2,1)}, u32[]{:S(2)}) copy-start(bf16[384,768]{1,0:T(8,128)(2,1)} %param.21) | copy-start | bytes 1769476
  271.5 20.4 %copy-start.35 = (f32[6,512]{1,0:T(8,128)S(1)}, f32[6,512]{1,0:T(8,128)}, u32[]{:S(2)}) copy-start(f32[6,512]{1,0:T(8,128)} %get-tuple-element.219) | copy-start | bytes 36868
  291.4 4.6 copy-start.18
  291.9 4.2 slice-start
  291.9 4.9 slice-start.1
  317.9 245.2 %all-reduce.7.cloned.1.call-start = ((), (), s32[]{:S(2)}) async-start(), calls=%async_computation.24 | async-start | bytes 22020096
  352.4 273.5 %reduce-scatter.33.cloned.1.call-start = ((), (), s32[]{:S(2)}) async-start(), calls=%async_computation.22 | async-start | bytes 1253376 | tf_op jit(solution)/shard_map/reduce_scatter | solution.py:336
  355.4 332.1 %reduce-scatter.31.cloned.1.call-start = ((), (), s32[]{:S(2)}) async-start(), calls=%async_computation.21 | async-start | bytes 1253376 | tf_op jit(solution)/shard_map/reduce_scatter | solution.py:334
  358.3 399.4 %reduce-scatter.35.cloned.1.call-start = ((), (), s32[]{:S(2)}) async-start(), calls=%async_computation.23 | async-start | bytes 3342336 | tf_op jit(solution)/shard_map/reduce_scatter | solution.py:338
  364.2 6.0 copy-start.56
  364.2 7.3 copy-start.38
  364.2 455.0 %reduce-scatter.29.cloned.1.call-start = ((), (), s32[]{:S(2)}) async-start(), calls=%async_computation.20 | async-start | bytes 1253376 | tf_op jit(solution)/shard_map/reduce_scatter | solution.py:333
  367.2 513.6 %reduce-scatter.27.cloned.1.call-start = ((), (), s32[]{:S(2)}) async-start(), calls=%async_computation.19 | async-start | bytes 1253376 | tf_op jit(solution)/shard_map/reduce_scatter | solution.py:331
  372.1 5.6 copy-start.39
  378.3 9.3 %copy-start.37 = (f32[256]{0:T(256)S(1)}, f32[256]{0:T(256)}, u32[]{:S(2)}) copy-start(f32[256]{0:T(256)} %copy-done.36) | copy-start | bytes 3076
  385.5 495.4 %copy-start.1 = (bf16[2,768,1024]{2,1,0:T(8,128)(2,1)S(1)}, bf16[2,768,1024]{2,1,0:T(8,128)(2,1)}, u32[]{:S(2)}) copy-start(bf16[2,768,1024]{2,1,0:T(8,128)(2,1)} %param.25) | copy-start | bytes 9437188
  (29 other events, 47.5 us)
Sparse Core Ops, SparseCore 0:
  67.5 29.3 reduce-scatter.12
  126.8 30.4 reduce-scatter.14
  181.2 17.6 reduce-scatter.18
  225.8 17.4 reduce-scatter.20
  245.3 26.0 reduce-scatter.16
  273.7 21.7 reduce-scatter.24
  318.0 17.4 reduce-scatter.22
  352.6 210.4 all-reduce.6
  567.7 58.1 reduce-scatter.32
  630.4 57.0 reduce-scatter.30
  692.4 65.2 reduce-scatter.34
  762.2 56.9 reduce-scatter.28
  823.8 57.0 reduce-scatter.26
